TPU v7x, 32 devices: a whole 2x2x4 slice. The times are simulated.
32 devices in a mesh: seq: 8 (over z, x), chan: 4 (over y, core).
Axes of the slice: x: 2, y: 2, z: 4, core: 2. Of those that a mesh axis runs over, the one named last changes fastest.
Arguments:
- signal: float32 [256, 65536], P('chan', 'seq'), may hold values from -6 to 6
- gating: float32 [256, 65536], P('chan', 'seq'), may hold values from -6 to 6
- response: float32 [256, 65536], P('chan', 'seq'), may hold values from -0.0234375 to 0.0234375
- skip_gain: float32 [256], P('chan'), may hold values from -4 to 4
- mixing_weight: float32 [256, 256], P(None, 'chan'), may hold values from -0.5 to 0.5
Outputs:
- output: float32 [256, 65536], P('chan', 'seq')
All inputs are finite; a program needn't handle non-finite values.
Results may differ from a plain program's by a relative error of at most 0.00007.
Values sent between devices are 32-bit elements; how exact they have to be, the bound alone decides.
A program may use at most 128 MiB of HBM per device.

v0:
```python
from functools import partial
import math
import jax
import jax.numpy as jnp
import numpy as np
from jax import lax
from jax.sharding import PartitionSpec as P


def twiddle(number, period):
    angle = (number % period).astype(jnp.float32) * (2.0 * math.pi / period)
    return (jnp.cos(angle), jnp.sin(angle))


def rotate(real_part, imag_part, cos_part, sin_part):
    return (
        real_part * cos_part - imag_part * sin_part,
        imag_part * cos_part + real_part * sin_part,
    )


def dft_table(length, sign):
    steps = jnp.arange(length, dtype=jnp.int32)
    cos_part, sin_part = twiddle(steps[:, None] * steps[None, :], length)
    return (cos_part, sign * sin_part)


def complex_apply(pattern, table_real, table_imag, real_part, imag_part):
    contract = partial(jnp.einsum, pattern, precision=lax.Precision.HIGHEST)
    return (
        contract(table_real, real_part) - contract(table_imag, imag_part),
        contract(table_real, imag_part) + contract(table_imag, real_part),
    )


def spectral_order(length):
    if length <= 256:
        return np.arange(length)
    outer_len = length // 128
    return (spectral_order(outer_len)[:, None] + outer_len * np.arange(128)[None, :]).reshape(-1)


def whole_forward(real_part, imag_part, length):
    if length <= 256:
        table_real, table_imag = dft_table(length, -1.0)
        return complex_apply("kn,...n->...k", table_real, table_imag, real_part, imag_part)
    inner_len = 128
    outer_len = length // inner_len
    lead = real_part.shape[:-1]
    real_part = jnp.swapaxes(real_part.reshape(lead + (outer_len, inner_len)), -1, -2)
    imag_part = jnp.swapaxes(imag_part.reshape(lead + (outer_len, inner_len)), -1, -2)
    real_part, imag_part = whole_forward(real_part, imag_part, outer_len)
    real_part = jnp.swapaxes(real_part, -1, -2)
    imag_part = jnp.swapaxes(imag_part, -1, -2)
    freq_idx = jnp.asarray(spectral_order(outer_len), dtype=jnp.int32)[:, None]
    inner_idx = jnp.arange(inner_len, dtype=jnp.int32)[None, :]
    cos_part, sin_part = twiddle(freq_idx * inner_idx, length)
    real_part, imag_part = rotate(real_part, imag_part, cos_part, -sin_part)
    table_real, table_imag = dft_table(inner_len, -1.0)
    real_part, imag_part = complex_apply(
        "ub,...tb->...tu", table_real, table_imag, real_part, imag_part
    )
    return (real_part.reshape(lead + (length,)), imag_part.reshape(lead + (length,)))


def whole_inverse(real_part, imag_part, length):
    if length <= 256:
        table_real, table_imag = dft_table(length, 1.0)
        return complex_apply("kn,...n->...k", table_real, table_imag, real_part, imag_part)
    inner_len = 128
    outer_len = length // inner_len
    lead = real_part.shape[:-1]
    real_part = real_part.reshape(lead + (outer_len, inner_len))
    imag_part = imag_part.reshape(lead + (outer_len, inner_len))
    table_real, table_imag = dft_table(inner_len, 1.0)
    real_part, imag_part = complex_apply(
        "bu,...tu->...tb", table_real, table_imag, real_part, imag_part
    )
    freq_idx = jnp.asarray(spectral_order(outer_len), dtype=jnp.int32)[:, None]
    inner_idx = jnp.arange(inner_len, dtype=jnp.int32)[None, :]
    cos_part, sin_part = twiddle(freq_idx * inner_idx, length)
    real_part, imag_part = rotate(real_part, imag_part, cos_part, sin_part)
    real_part, imag_part = whole_inverse(
        jnp.swapaxes(real_part, -1, -2), jnp.swapaxes(imag_part, -1, -2), outer_len
    )
    real_part = jnp.swapaxes(real_part, -1, -2)
    imag_part = jnp.swapaxes(imag_part, -1, -2)
    return (real_part.reshape(lead + (length,)), imag_part.reshape(lead + (length,)))


def owner_conv(stacked, groups, samples):
    chan_rows = stacked.shape[1]
    own_rows = chan_rows // groups
    span = groups * samples
    pieces = stacked.reshape(2, groups, own_rows, samples)
    rows_whole = lax.all_to_all(pieces, "seq", split_axis=1, concat_axis=3, tiled=True).reshape(
        2, own_rows, span
    )
    padded = jnp.concatenate([rows_whole, jnp.zeros_like(rows_whole)], axis=2)
    spec_real, spec_imag = whole_forward(padded, jnp.zeros_like(padded), 2 * span)
    prod_real = spec_real[0] * spec_real[1] - spec_imag[0] * spec_imag[1]
    prod_imag = spec_real[0] * spec_imag[1] + spec_imag[0] * spec_real[1]
    back_real, back_imag = whole_inverse(prod_real, prod_imag, 2 * span)
    conv_rows = back_real[:, :span]
    return lax.all_to_all(conv_rows, "seq", split_axis=1, concat_axis=0, tiled=True)


def per_device(signal, gating, response, skip_gain, mixing_weight):
    chan_rows, samples = signal.shape
    groups = lax.axis_size("seq")
    full_len = 2 * groups * samples
    stacked = jnp.stack([signal, response])
    conv = owner_conv(stacked, groups, samples)
    conv = conv / full_len
    mixed_in = gating * (conv + skip_gain[:, None] * signal)
    return lax.psum_scatter(
        jnp.dot(
            mixing_weight,
            mixed_in,
            precision=lax.Precision.HIGHEST,
            preferred_element_type=jnp.float32,
        ),
        "chan",
        scatter_dimension=0,
        tiled=True,
    )


def solution(mesh):
    in_specs = (P("chan", "seq"), P("chan", "seq"), P("chan", "seq"), P("chan"), P(None, "chan"))
    out_specs = P("chan", "seq")
    return jax.shard_map(
        per_device, mesh=mesh, in_specs=in_specs, out_specs=out_specs, check_vma=False
    )
```

profile of v0, /device:TPU:0, one launch (start us, length us, event | category | flops | bytes accessed | tf_op | source)
XLA Modules:
  0.0 486.4 jit_solution(6807660299492079792)
XLA Ops:
  6.5 4.6 pad_maximum_fusion
  11.1 7.4 %all-to-all-start = ((f32[2,8,8,8192]{3,2,0,1:T(8,128)}), f32[2,8,8,8192]{3,2,0,1:T(8,128)}, u32[]{:S(2)}, u32[]{:S(2)}) async-start(f32[2,8,8,8192]{3,2,0,1:T(8,128)} %pad_maximum_fusion), calls=%async_computation | async-start | bytes 8388608 | tf_op jit(solution)/shard_map/all_to_all | solution.py:96
  24.3 8.9 %fusion.34 = f32[2,8,128,128,8]{3,4,2,1,0:T(8,128)} fusion(), kind=kOutput, calls=%fused_computation.58 | convolution fusion | flops 201327552 | bytes 8388608 | tf_op jit(solution)/shard_map/kn,...n->...k/dot_general | solution.py:31
  33.2 78.7 %all-to-all-done = f32[2,8,8,8192]{3,2,0,1:T(8,128)} async-done(((f32[2,8,8,8192]{3,2,0,1:T(8,128)}), f32[2,8,8,8192]{3,2,0,1:T(8,128)}, u32[]{:S(2)}, u32[]{:S(2)}) %all-to-all-start) | async-done | bytes 4194336 | tf_op jit(solution)/shard_map/all_to_all | solution.py:96
  111.8 6.6 %copy.47 = f32[2,1,8,8,8192]{4,3,2,0,1:T(8,128)} copy(f32[2,1,8,8,8192]{4,2,0,3,1:T(8,128)} %bitcast.3) | data formatting | bytes 8388608 | tf_op jit(solution)/shard_map/all_to_all | solution.py:96
  125.1 4.9 %copy.100 = f32[2,8,1024,128]{3,2,1,0:T(8,128)} copy(f32[2,8,1024,128]{3,1,2,0:T(8,128)S(1)} %pad_bitcast_fusion) | data formatting | bytes 16777216
  130.0 8.7 %copy.74 = f32[2,8,128,8,128]{4,3,2,1,0:T(8,128)} copy(f32[2,8,128,8,128]{2,4,3,1,0:T(8,128)} %bitcast.216) | data formatting | bytes 16777216 | tf_op jit(solution)/shard_map/reshape | solution.py:50
  138.6 12.5 %fusion.4 = f32[2,8,128,128,8]{3,4,2,1,0:T(8,128)} fusion(f32[2,8,128,8,128]{4,3,2,1,0:T(8,128)} %copy.74), kind=kOutput, calls=%fused_computation.14 | convolution fusion | flops 201327552 | bytes 16777216 | tf_op jit(solution)/shard_map/kn,...n->...k/dot_general | solution.py:32
  151.1 9.3 %fusion.6 = f32[2,8,128,128,8]{3,4,2,1,0:T(8,128)} fusion(f32[2,8,128,8,128]{4,3,2,1,0:T(8,128)S(1)} %copy-done.1), kind=kOutput, calls=%fused_computation.16 | convolution fusion | flops 201327488 | bytes 16777216 | tf_op jit(solution)/shard_map/kn,...n->...k/dot_general | solution.py:31
  160.4 15.3 %fusion.2 = (f32[2,8,128,8,128]{4,3,2,1,0:T(8,128)}, f32[2,8,128,8,128]{4,3,2,1,0:T(8,128)S(1)}) fusion(f32[8,128]{1,0:T(8,128)S(1)} %get-tuple-element.19, f32[8,128]{1,0:T(8,128)S(1)} %get-tuple-element.20, f32[2,8,128,128,8]{3,4,2,1,0:T(8,128)} %fusion.4, f32[2,8,128,128,8]{3,4,2,1,0:T(8,128)} %fusion.6, f32[2,8,128,128,8]{3,4,2,1,0:T(8,128)} %fusion.34), kind=kOutput, calls=%fused_computation.10 | convolution fusion | flops 218104704 | bytes 41951232 | tf_op jit(solution)/shard_map/kn,...n->...k/dot_general | solution.py:32
  175.7 11.1 %fusion.8 = f32[2,8,128,8,128]{2,4,3,1,0:T(8,128)} fusion(f32[2,8,128,8,128]{4,3,2,1,0:T(8,128)S(1)} %get-tuple-element.6), kind=kOutput, calls=%fused_computation.19 | convolution fusion | flops 3221454848 | bytes 16777216 | tf_op jit(solution)/shard_map/ub,...tb->...tu/dot_general | solution.py:32
  186.8 8.8 %fusion.10 = f32[2,8,128,8,128]{2,4,3,1,0:T(8,128)S(1)} fusion(f32[2,8,128,8,128]{4,3,2,1,0:T(8,128)S(1)} %get-tuple-element.6), kind=kOutput, calls=%fused_computation.21 | convolution fusion | flops 3221471232 | bytes 16777216 | tf_op jit(solution)/shard_map/ub,...tb->...tu/dot_general | solution.py:31
  195.7 13.0 %fusion.39 = f32[2,8,128,8,128]{2,4,3,1,0:T(8,128)} fusion(f32[2,8,128,8,128]{2,4,3,1,0:T(8,128)} %fusion.8, f32[2,8,128,8,128]{4,3,2,1,0:T(8,128)S(1)} %bitcast.211), kind=kOutput, calls=%fused_computation.61 | convolution fusion | flops 3223568384 | bytes 25165824 | tf_op jit(solution)/shard_map/ub,...tb->...tu/dot_general | solution.py:32
  208.7 10.7 %fusion.36 = f32[2,8,128,8,128]{2,4,3,1,0:T(8,128)} fusion(f32[2,8,128,8,128]{2,4,3,1,0:T(8,128)S(1)} %fusion.10, f32[2,8,128,8,128]{4,3,2,1,0:T(8,128)S(1)} %bitcast.211), kind=kOutput, calls=%fused_computation.60 | convolution fusion | flops 3223552000 | bytes 25165824 | tf_op jit(solution)/shard_map/ub,...tb->...tu/dot_general | solution.py:31
  219.4 7.0 %fusion = (f32[2,8,1024,128]{3,2,1,0:T(8,128)S(1)}, f32[2,8,1024,128]{3,2,1,0:T(8,128)S(1)}) fusion(f32[2,8,128,8,128]{2,4,3,1,0:T(8,128)} %fusion.36, f32[2,8,128,8,128]{2,4,3,1,0:T(8,128)} %fusion.39, f32[1024,128]{1,0:T(8,128)S(1)} %get-tuple-element.18, f32[1024,128]{1,0:T(8,128)S(1)} %get-tuple-element.17), kind=kLoop, calls=%fused_computation.4 | loop fusion | flops 12582912 | bytes 34603008 | tf_op jit(solution)/shard_map/sub | solution.py:17
  226.5 9.7 %fusion.88 = f32[2,8,1024,128]{3,2,1,0:T(8,128)} fusion(f32[2,8,1024,128]{3,2,1,0:T(8,128)S(1)} %get-tuple-element.7), kind=kOutput, calls=%fused_computation.116 | convolution fusion | flops 3221454848 | bytes 16777216 | tf_op jit(solution)/shard_map/ub,...tb->...tu/dot_general | solution.py:31
  236.2 7.8 %fusion.86 = f32[2,8,1024,128]{3,2,1,0:T(8,128)S(1)} fusion(f32[2,8,1024,128]{3,2,1,0:T(8,128)S(1)} %get-tuple-element.8), kind=kOutput, calls=%fused_computation.114 | convolution fusion | flops 3221454848 | bytes 16777216 | tf_op jit(solution)/shard_map/ub,...tb->...tu/dot_general | solution.py:32
  244.0 11.4 %convolution_subtract_fusion = f32[2,8,1024,128]{3,2,1,0:T(8,128)} fusion(f32[2,8,1024,128]{3,2,1,0:T(8,128)} %fusion.88, f32[2,8,1024,128]{3,2,1,0:T(8,128)S(1)} %get-tuple-element.8), kind=kOutput, calls=%fused_computation.63 | convolution fusion | flops 3223568384 | bytes 25165824 | tf_op jit(solution)/shard_map/ub,...tb->...tu/dot_general | solution.py:31
  255.4 9.5 %convolution_add_fusion = f32[2,8,1024,128]{3,2,1,0:T(8,128)} fusion(f32[2,8,1024,128]{3,2,1,0:T(8,128)S(1)} %fusion.86, f32[2,8,1024,128]{3,2,1,0:T(8,128)S(1)} %get-tuple-element.7), kind=kOutput, calls=%fused_computation.62 | convolution fusion | flops 3223568384 | bytes 25165824 | tf_op jit(solution)/shard_map/ub,...tb->...tu/dot_general | solution.py:32
  280.6 5.2 %fusion.18 = (f32[8,128,1024]{1,2,0:T(8,128)S(1)}, f32[8,128,1024]{1,2,0:T(8,128)S(1)}) fusion(f32[8,1024,128]{2,1,0:T(8,128)S(1)} %fusion.44, f32[128,1024]{0,1:T(8,128)S(1)} %copy-done.5, f32[128,1024]{0,1:T(8,128)S(1)} %copy-done.4, f32[8,1024,128]{2,1,0:T(8,128)S(1)} %fusion.20, f32[1,8,1024,128]{3,2,1,0:T(8,128)S(1)} %get-tuple-element.9), kind=kOutput, calls=%fused_computation.37 | convolution fusion | flops 1618182144 | bytes 22020096 | tf_op jit(solution)/shard_map/bu,...tu->...tb/dot_general | solution.py:32
  285.9 7.0 %fusion.84 = f32[8,128,8,128]{3,1,2,0:T(8,128)S(1)} fusion(f32[8,128,8,128]{1,3,2,0:T(8,128)S(1)} %bitcast.212), kind=kOutput, calls=%fused_computation.112 | convolution fusion | flops 1610842112 | bytes 8388608 | tf_op jit(solution)/shard_map/bu,...tu->...tb/dot_general | solution.py:31
  292.9 7.3 %fusion.82 = f32[8,128,8,128]{3,1,2,0:T(8,128)S(1)} fusion(f32[8,128,8,128]{1,3,2,0:T(8,128)S(1)} %bitcast.214), kind=kOutput, calls=%fused_computation.110 | convolution fusion | flops 1610842112 | bytes 8388608 | tf_op jit(solution)/shard_map/bu,...tu->...tb/dot_general | solution.py:32
  300.2 7.1 %convolution_subtract_fusion.1 = f32[8,128,8,128]{3,1,2,0:T(8,128)S(1)} fusion(f32[8,128,8,128]{3,1,2,0:T(8,128)S(1)} %fusion.84, f32[8,128,8,128]{1,3,2,0:T(8,128)S(1)} %bitcast.215), kind=kOutput, calls=%fused_computation.67 | convolution fusion | flops 1611890688 | bytes 12582912 | tf_op jit(solution)/shard_map/bu,...tu->...tb/dot_general | solution.py:31
  307.3 7.3 %fusion.16 = (f32[8,128,128,8]{2,1,3,0:T(8,128)S(1)}, f32[8,128,128,8]{2,1,3,0:T(8,128)S(1)}) fusion(f32[8,128,8,128]{3,1,2,0:T(8,128)S(1)} %convolution_subtract_fusion.1, f32[128,8]{0,1:T(8,128)S(1)} %get-tuple-element.21, f32[128,8]{0,1:T(8,128)S(1)} %get-tuple-element.22, f32[8,128,8,128]{3,1,2,0:T(8,128)S(1)} %fusion.82, ...), kind=kOutput, calls=%fused_computation.31 | convolution fusion | flops 1618182144 | bytes 20979712 | tf_op jit(solution)/shard_map/bu,...tu->...tb/dot_general | solution.py:32
  314.6 6.6 %fusion.28 = f32[8,128,128,8]{2,3,1,0:T(8,128)S(1)} fusion(f32[8,128,128,8]{2,1,3,0:T(8,128)S(1)} %get-tuple-element.14), kind=kOutput, calls=%fused_computation.49 | convolution fusion | flops 100664192 | bytes 8388608 | tf_op jit(solution)/shard_map/kn,...n->...k/dot_general | solution.py:31
  321.2 6.9 %subtract_bitcast_fusion = f32[8,128,8,128]{3,2,1,0:T(8,128)} fusion(f32[8,128,128,8]{2,3,1,0:T(8,128)S(1)} %fusion.28, f32[8,128,128,8]{2,1,3,0:T(8,128)S(1)} %get-tuple-element.13), kind=kOutput, calls=%fused_computation.53 | convolution fusion | flops 101712768 | bytes 12582912 | tf_op jit(solution)/shard_map/kn,...n->...k/dot_general | solution.py:31
  328.1 5.4 %copy.75 = f32[8,128,8,128]{1,3,2,0:T(8,128)} copy(f32[8,128,8,128]{3,2,1,0:T(8,128)} %subtract_bitcast_fusion) | data formatting | bytes 8388608 | tf_op jit(solution)/shard_map/reshape | solution.py:88
  333.5 4.6 copy.101
  338.3 52.3 %all_to_all.28 = f32[8,8,8192]{2,0,1:T(8,128)S(1)} all-to-all(f32[8,8,8192]{2,0,1:T(8,128)S(1)} %bitcast.219), channel_id=1, replica_groups=mesh['seq'=8,'chan'=4] {'seq'}, dimensions={1} | all-to-all | bytes 4194304 | tf_op jit(solution)/shard_map/all_to_all | solution.py:105
  390.6 9.1 %convolution_bitcast_fusion = f32[256,8192]{0,1:T(8,128)} fusion(f32[256,64]{0,1:T(8,128)S(1)} %copy-done, f32[64,8192]{1,0:T(8,128)S(1)} %copy-done.6, f32[64,8192]{1,0:T(8,128)S(1)} %copy-done.3, f32[8,8,8192]{2,0,1:T(8,128)S(1)} %all_to_all.28, f32[64]{0:T(128)S(1)} %copy-done.8), kind=kOutput, calls=%fused_computation | convolution fusion | flops 1612709888 | bytes 14745856 | tf_op jit(solution)/shard_map/dot_general | solution.py:117
  399.7 8.9 %copy.76 = f32[256,8192]{1,0:T(8,128)} copy(f32[256,8192]{0,1:T(8,128)} %convolution_bitcast_fusion) | data formatting | bytes 16777216
  408.6 70.6 %reduce-scatter.4.cloned.1.call-done = f32[64,8192]{1,0:T(8,128)} async-done(((f32[256,8192]{1,0:T(8,128)}), f32[64,8192]{1,0:T(8,128)}) %reduce-scatter.4.cloned.1.call-update) | async-done | bytes 2097168 | tf_op jit(solution)/shard_map/reduce_scatter | solution.py:116
  (36 shorter events, 28.2 us)
Async XLA Ops:
  6.5 384.1 %copy-start = (f32[256,64]{0,1:T(8,128)S(1)}, f32[256,64]{0,1:T(8,128)}, u32[]{:S(2)}) copy-start(f32[256,64]{0,1:T(8,128)} %param.13) | copy-start | bytes 196612
  11.1 7.6 %copy-start.7 = (s32[1024]{0:T(1024)S(1)}, s32[1024]{0:T(1024)}, u32[]{:S(2)}) copy-start(s32[1024]{0:T(1024)} %constant.100.clone) | copy-start | bytes 12292
  11.1 100.7 %all-to-all-start = ((f32[2,8,8,8192]{3,2,0,1:T(8,128)}), f32[2,8,8,8192]{3,2,0,1:T(8,128)}, u32[]{:S(2)}, u32[]{:S(2)}) async-start(f32[2,8,8,8192]{3,2,0,1:T(8,128)} %pad_maximum_fusion), calls=%async_computation | async-start | bytes 8388608 | tf_op jit(solution)/shard_map/all_to_all | solution.py:96
  18.6 460.7 %reduce-scatter.4.cloned.1.call-start = ((), (), s32[]{:S(2)}) async-start(), calls=%async_computation.3 | async-start | bytes 10485760 | tf_op jit(solution)/shard_map/reduce_scatter | solution.py:116
  138.6 12.5 %copy-start.1 = (f32[2,8,128,8,128]{4,3,2,1,0:T(8,128)S(1)}, f32[2,8,128,8,128]{4,3,2,1,0:T(8,128)}, u32[]{:S(2)}) copy-start(f32[2,8,128,8,128]{4,3,2,1,0:T(8,128)} %copy.74) | copy-start | bytes 25165828
  175.7 20.0 %slice-start = ((s8[8388608]{0:T(1024)(128)(4,1)}), s8[4194304]{0:T(1024)(128)(4,1)S(1)}, s32[]{:S(2)}) async-start(s8[8388608]{0:T(1024)(128)(4,1)} %bitcast.210), calls=%async_computation.4 | async-start | bytes 8388608
  186.8 8.9 %slice-start.1 = ((s8[8388608]{0:T(1024)(128)(4,1)}), s8[4194304]{0:T(1024)(128)(4,1)S(1)}, s32[]{:S(2)}) async-start(s8[8388608]{0:T(1024)(128)(4,1)} %bitcast.210), calls=%async_computation.5 | async-start | bytes 8388608
  255.4 9.5 %copy-start.2 = (f32[2,8,1024,128]{3,2,1,0:T(8,128)S(1)}, f32[2,8,1024,128]{3,2,1,0:T(8,128)}, u32[]{:S(2)}) copy-start(f32[2,8,1024,128]{3,2,1,0:T(8,128)} %convolution_subtract_fusion) | copy-start | bytes 25165828
  276.8 3.9 copy-start.4
  276.8 3.9 copy-start.5
  338.1 52.5 %copy-start.3 = (f32[64,8192]{1,0:T(8,128)S(1)}, f32[64,8192]{1,0:T(8,128)}, u32[]{:S(2)}) copy-start(f32[64,8192]{1,0:T(8,128)} %param.9) | copy-start | bytes 6291460
  338.1 52.5 %copy-start.6 = (f32[64,8192]{1,0:T(8,128)S(1)}, f32[64,8192]{1,0:T(8,128)}, u32[]{:S(2)}) copy-start(f32[64,8192]{1,0:T(8,128)} %param.10) | copy-start | bytes 6291460
  338.1 52.5 %copy-start.8 = (f32[64]{0:T(128)S(1)}, f32[64]{0:T(128)}, u32[]{:S(2)}) copy-start(f32[64]{0:T(128)} %param.12) | copy-start | bytes 772
Sparse Core Ops, SparseCore 0:
  408.8 70.4 reduce-scatter.3
where the time goes:
time: 490 us; the launch traced here: 486 us
  matrix products  196 us (40%)
  waiting for transfers between devices  149 us (30%)
  blocking collectives  52.3 us (11%)
  local copies, waits for them, and re-layouts  45.9 us (9%)
  other arithmetic  21.5 us (4%)
  between operations  13.9 us (3%)
  starting transfers between devices  7.45 us (2%)
    all_to_all x1, waiting for transfers between devices, owner_conv(): lax.all_to_all(pieces, 'seq', split_axis=1, concat_axis=3, tiled=True)  78.7 us
    reduce_scatter x1, waiting for transfers between devices, per_device(): lax.psum_scatter(jnp.dot(mixing_weight, mixed_in, precision=lax.Precision...  70.6 us
    all_to_all x1, blocking collectives, owner_conv(): lax.all_to_all(conv_rows, 'seq', split_axis=1, concat_axis=0, tiled=True)  52.3 us
    dot_general x5, matrix products, complex_apply(): contract(table_imag, real_part)  47.6 us
    dot_general x6, matrix products, complex_apply(): contract(table_real, real_part) - contract(table_imag, imag_part)  47.5 us
    dot_general x6, matrix products, complex_apply(): contract(table_imag, imag_part)  46.6 us
    dot_general x5, matrix products, complex_apply(): contract(table_real, imag_part) + contract(table_imag, real_part)  45.3 us
    unnamed x26, local copies, waits for them, and re-layouts  21.2 us
  transfers between devices with their start and end apart: 2, of which 2 were waited for; matrix products, arithmetic and copies ran while one was open for 3% of the time, Pallas kernels for 0%

commit v1 on v0

--- a/solution.py
+++ b/solution.py
@@ -5,6 +5,24 @@
 import numpy as np
 from jax import lax
 from jax.sharding import PartitionSpec as P
+
+
+def slots_process(x0, comm_axis):
+    field_out = lax.axis_size(comm_axis)
+    near = lax.axis_index(comm_axis)
+    new, t_next = (field_out, near)
+    arr_now = x0.shape[1] // new
+    piece_next = list(x0.shape)
+    piece_next[1] = arr_now
+    m_next = piece_next[3]
+    piece_next[3] = m_next * new
+    upper = jnp.zeros(piece_next, x0.dtype)
+    for k in range(new):
+        ready = lax.dynamic_slice_in_dim(x0, (t_next ^ k) * arr_now, arr_now, axis=1)
+        if k:
+            ready = lax.ppermute(ready, comm_axis, [(jj, jj ^ k) for jj in range(new)])
+        upper = lax.dynamic_update_slice_in_dim(upper, ready, (t_next ^ k) * m_next, axis=3)
+    return upper
 
 
 def twiddle(number, period):
@@ -93,9 +111,7 @@
     own_rows = chan_rows // groups
     span = groups * samples
     pieces = stacked.reshape(2, groups, own_rows, samples)
-    rows_whole = lax.all_to_all(pieces, "seq", split_axis=1, concat_axis=3, tiled=True).reshape(
-        2, own_rows, span
-    )
+    rows_whole = slots_process(pieces, comm_axis="seq").reshape(2, own_rows, span)
     padded = jnp.concatenate([rows_whole, jnp.zeros_like(rows_whole)], axis=2)
     spec_real, spec_imag = whole_forward(padded, jnp.zeros_like(padded), 2 * span)
     prod_real = spec_real[0] * spec_real[1] - spec_imag[0] * spec_imag[1]

time: 490 us -> 473 us (0.965)
  waiting for transfers between devices: 149 us -> 113 us
  blocking collectives: 52.3 us -> 70.2 us
  starting transfers between devices: 7.45 us -> 13.4 us
  local copies, waits for them, and re-layouts: 45.9 us -> 40.4 us
    all_to_all x1 -> x0, waiting for transfers between devices: 78.7 us -> none  [owner_conv(): lax.all_to_all(pieces, 'seq', split_axis=1, concat_axis=3, tiled=True)]
    ppermute x0 -> x7, waiting for transfers between devices: none -> 42.3 us  [slots_process(): ready = lax.ppermute(ready, comm_axis, [(jj, jj ^ k) for jj in range(new)])]
    all_to_all x1, blocking collectives: 52.3 us -> 70.2 us  [owner_conv(): lax.all_to_all(conv_rows, 'seq', split_axis=1, concat_axis=0, tiled=True)]
    ppermute x0 -> x7, starting transfers between devices: none -> 13.4 us  [slots_process(): ready = lax.ppermute(ready, comm_axis, [(jj, jj ^ k) for jj in range(new)])]
    all_to_all x1 -> x0, starting transfers between devices: 7.41 us -> none  [owner_conv(): lax.all_to_all(pieces, 'seq', split_axis=1, concat_axis=3, tiled=True)]
    all_to_all x1 -> x0, local copies, waits for them, and re-layouts: 6.56 us -> none  [owner_conv(): lax.all_to_all(pieces, 'seq', split_axis=1, concat_axis=3, tiled=True)]
    dynamic_update_slice x0 -> x7, local copies, waits for them, and re-layouts: none -> 5.47 us  [slots_process(): lax.dynamic_update_slice_in_dim(upper, ready, (t_next ^ k) * m_next, axis=3)]
    unnamed x26 -> x34, local copies, waits for them, and re-layouts: 21.2 us -> 20.4 us
  transfers between devices with their start and end apart: 2 -> 8, of which waited for: 2 -> 4; matrix products, arithmetic and copies ran while one was open for 3% -> 5% of each run, Pallas kernels for 0% -> 0%
where the time goes in v1:
time: 473 us; the launch traced here: 469 us
  matrix products  196 us (41%)
  waiting for transfers between devices  113 us (24%)
  blocking collectives  70.2 us (15%)
  local copies, waits for them, and re-layouts  40.4 us (9%)
  other arithmetic  22.4 us (5%)
  between operations  14 us (3%)
  starting transfers between devices  13.4 us (3%)
    reduce_scatter x1, waiting for transfers between devices, per_device(): lax.psum_scatter(jnp.dot(mixing_weight, mixed_in, precision=lax.Precision...  70.6 us
    all_to_all x1, blocking collectives, owner_conv(): lax.all_to_all(conv_rows, 'seq', split_axis=1, concat_axis=0, tiled=True)  70.2 us
    dot_general x6, matrix products, complex_apply(): contract(table_real, real_part) - contract(table_imag, imag_part)  47.8 us
    dot_general x5, matrix products, complex_apply(): contract(table_imag, real_part)  47.4 us
    dot_general x6, matrix products, complex_apply(): contract(table_imag, imag_part)  46.6 us
    dot_general x5, matrix products, complex_apply(): contract(table_real, imag_part) + contract(table_imag, real_part)  45 us
    ppermute x7, waiting for transfers between devices, slots_process(): ready = lax.ppermute(ready, comm_axis, [(jj, jj ^ k) for jj in range(new)])  42.3 us
    unnamed x34, local copies, waits for them, and re-layouts  20.4 us
  transfers between devices with their start and end apart: 8, of which 4 were waited for; matrix products, arithmetic and copies ran while one was open for 5% of the time, Pallas kernels for 0%

profile of v1, /device:TPU:0, one launch (start us, length us, event | category | flops | bytes accessed | tf_op | source)
XLA Modules:
  0.0 469.1 jit_solution(389231470516018859)
XLA Ops:
  28.2 8.9 %fusion.34 = f32[2,8,128,128,8]{3,4,2,1,0:T(8,128)} fusion(), kind=kOutput, calls=%fused_computation.73 | convolution fusion | flops 201327552 | bytes 8388608 | tf_op jit(solution)/shard_map/kn,...n->...k/dot_general | solution.py:49
  41.8 8.2 %collective-permute-done.1 = f32[2,1,8,8192]{3,2,0,1:T(8,128)} collective-permute-done((f32[2,1,8,8192]{3,2,0,1:T(8,128)}, f32[2,1,8,8192]{3,2,0,1:T(8,128)}, u32[]{:S(2)}, u32[]{:S(2)}) %collective-permute-start.1) | collective-permute-done | bytes 524320 | tf_op jit(solution)/shard_map/ppermute | solution.py:23
  52.0 6.9 %collective-permute-done.2 = f32[2,1,8,8192]{3,2,0,1:T(8,128)} collective-permute-done((f32[2,1,8,8192]{3,2,0,1:T(8,128)}, f32[2,1,8,8192]{3,2,0,1:T(8,128)}, u32[]{:S(2)}, u32[]{:S(2)}) %collective-permute-start.2) | collective-permute-done | bytes 524320 | tf_op jit(solution)/shard_map/ppermute | solution.py:23
  61.0 27.3 %collective-permute-done.4 = f32[2,1,8,8192]{3,2,0,1:T(8,128)} collective-permute-done((f32[2,1,8,8192]{3,2,0,1:T(8,128)}, f32[2,1,8,8192]{3,2,0,1:T(8,128)}, u32[]{:S(2)}, u32[]{:S(2)}) %collective-permute-start.4) | collective-permute-done | bytes 524320 | tf_op jit(solution)/shard_map/ppermute | solution.py:23
  90.1 4.9 %copy.90 = f32[2,8,1024,128]{3,2,1,0:T(8,128)} copy(f32[2,8,1024,128]{3,1,2,0:T(8,128)S(1)} %pad_bitcast_fusion) | data formatting | bytes 16777216
  95.0 8.7 %copy.64 = f32[2,8,128,8,128]{4,3,2,1,0:T(8,128)} copy(f32[2,8,128,8,128]{2,4,3,1,0:T(8,128)} %bitcast.234) | data formatting | bytes 16777216 | tf_op jit(solution)/shard_map/reshape | solution.py:68
  103.7 12.3 %fusion.4 = f32[2,8,128,128,8]{3,4,2,1,0:T(8,128)} fusion(f32[2,8,128,8,128]{4,3,2,1,0:T(8,128)} %copy.64), kind=kOutput, calls=%fused_computation.30 | convolution fusion | flops 201327552 | bytes 16777216 | tf_op jit(solution)/shard_map/kn,...n->...k/dot_general | solution.py:50
  115.9 9.5 %fusion.6 = f32[2,8,128,128,8]{3,4,2,1,0:T(8,128)} fusion(f32[2,8,128,8,128]{4,3,2,1,0:T(8,128)S(1)} %copy-done.1), kind=kOutput, calls=%fused_computation.32 | convolution fusion | flops 201327488 | bytes 16777216 | tf_op jit(solution)/shard_map/kn,...n->...k/dot_general | solution.py:49
  125.4 15.1 %fusion.2 = (f32[2,8,128,8,128]{4,3,2,1,0:T(8,128)}, f32[2,8,128,8,128]{4,3,2,1,0:T(8,128)S(1)}) fusion(f32[8,128]{1,0:T(8,128)S(1)} %get-tuple-element.25, f32[8,128]{1,0:T(8,128)S(1)} %get-tuple-element.26, f32[2,8,128,128,8]{3,4,2,1,0:T(8,128)} %fusion.4, f32[2,8,128,128,8]{3,4,2,1,0:T(8,128)} %fusion.6, f32[2,8,128,128,8]{3,4,2,1,0:T(8,128)} %fusion.34), kind=kOutput, calls=%fused_computation.26 | convolution fusion | flops 218104704 | bytes 41951232 | tf_op jit(solution)/shard_map/kn,...n->...k/dot_general | solution.py:50
  140.5 11.0 %fusion.8 = f32[2,8,128,8,128]{2,4,3,1,0:T(8,128)} fusion(f32[2,8,128,8,128]{4,3,2,1,0:T(8,128)S(1)} %get-tuple-element.6), kind=kOutput, calls=%fused_computation.35 | convolution fusion | flops 3221454848 | bytes 16777216 | tf_op jit(solution)/shard_map/ub,...tb->...tu/dot_general | solution.py:50
  151.6 8.8 %fusion.10 = f32[2,8,128,8,128]{2,4,3,1,0:T(8,128)S(1)} fusion(f32[2,8,128,8,128]{4,3,2,1,0:T(8,128)S(1)} %get-tuple-element.6), kind=kOutput, calls=%fused_computation.37 | convolution fusion | flops 3221471232 | bytes 16777216 | tf_op jit(solution)/shard_map/ub,...tb->...tu/dot_general | solution.py:49
  160.4 13.0 %fusion.39 = f32[2,8,128,8,128]{2,4,3,1,0:T(8,128)} fusion(f32[2,8,128,8,128]{2,4,3,1,0:T(8,128)} %fusion.8, f32[2,8,128,8,128]{4,3,2,1,0:T(8,128)S(1)} %bitcast.226), kind=kOutput, calls=%fused_computation.76 | convolution fusion | flops 3223568384 | bytes 25165824 | tf_op jit(solution)/shard_map/ub,...tb->...tu/dot_general | solution.py:50
  173.5 10.7 %fusion.36 = f32[2,8,128,8,128]{2,4,3,1,0:T(8,128)} fusion(f32[2,8,128,8,128]{2,4,3,1,0:T(8,128)S(1)} %fusion.10, f32[2,8,128,8,128]{4,3,2,1,0:T(8,128)S(1)} %bitcast.226), kind=kOutput, calls=%fused_computation.75 | convolution fusion | flops 3223552000 | bytes 25165824 | tf_op jit(solution)/shard_map/ub,...tb->...tu/dot_general | solution.py:49
  184.2 7.0 %fusion = (f32[2,8,1024,128]{3,2,1,0:T(8,128)S(1)}, f32[2,8,1024,128]{3,2,1,0:T(8,128)S(1)}) fusion(f32[2,8,128,8,128]{2,4,3,1,0:T(8,128)} %fusion.36, f32[2,8,128,8,128]{2,4,3,1,0:T(8,128)} %fusion.39, f32[1024,128]{1,0:T(8,128)S(1)} %get-tuple-element.24, f32[1024,128]{1,0:T(8,128)S(1)} %get-tuple-element.23), kind=kLoop, calls=%fused_computation.20 | loop fusion | flops 12582912 | bytes 34603008 | tf_op jit(solution)/shard_map/sub | solution.py:35
  191.2 9.8 %fusion.98 = f32[2,8,1024,128]{3,2,1,0:T(8,128)} fusion(f32[2,8,1024,128]{3,2,1,0:T(8,128)S(1)} %get-tuple-element.7), kind=kOutput, calls=%fused_computation.148 | convolution fusion | flops 3221454848 | bytes 16777216 | tf_op jit(solution)/shard_map/ub,...tb->...tu/dot_general | solution.py:49
  201.0 7.8 %fusion.96 = f32[2,8,1024,128]{3,2,1,0:T(8,128)S(1)} fusion(f32[2,8,1024,128]{3,2,1,0:T(8,128)S(1)} %get-tuple-element.8), kind=kOutput, calls=%fused_computation.146 | convolution fusion | flops 3221454848 | bytes 16777216 | tf_op jit(solution)/shard_map/ub,...tb->...tu/dot_general | solution.py:50
  208.8 11.4 %convolution_subtract_fusion = f32[2,8,1024,128]{3,2,1,0:T(8,128)} fusion(f32[2,8,1024,128]{3,2,1,0:T(8,128)} %fusion.98, f32[2,8,1024,128]{3,2,1,0:T(8,128)S(1)} %get-tuple-element.8), kind=kOutput, calls=%fused_computation.78 | convolution fusion | flops 3223568384 | bytes 25165824 | tf_op jit(solution)/shard_map/ub,...tb->...tu/dot_general | solution.py:49
  220.2 9.6 %convolution_add_fusion = f32[2,8,1024,128]{3,2,1,0:T(8,128)} fusion(f32[2,8,1024,128]{3,2,1,0:T(8,128)S(1)} %fusion.96, f32[2,8,1024,128]{3,2,1,0:T(8,128)S(1)} %get-tuple-element.7), kind=kOutput, calls=%fused_computation.77 | convolution fusion | flops 3223568384 | bytes 25165824 | tf_op jit(solution)/shard_map/ub,...tb->...tu/dot_general | solution.py:50
  229.7 4.2 multiply_subtract_fusion
  245.5 5.2 %fusion.18 = (f32[8,128,1024]{1,2,0:T(8,128)S(1)}, f32[8,128,1024]{1,2,0:T(8,128)S(1)}) fusion(f32[8,1024,128]{2,1,0:T(8,128)S(1)} %fusion.44, f32[128,1024]{0,1:T(8,128)S(1)} %copy-done.7, f32[128,1024]{0,1:T(8,128)S(1)} %copy-done.6, f32[8,1024,128]{2,1,0:T(8,128)S(1)} %fusion.20, f32[1,8,1024,128]{3,2,1,0:T(8,128)S(1)} %get-tuple-element.9), kind=kOutput, calls=%fused_computation.52 | convolution fusion | flops 1618182144 | bytes 22020096 | tf_op jit(solution)/shard_map/bu,...tu->...tb/dot_general | solution.py:50
  250.7 7.0 %fusion.94 = f32[8,128,8,128]{3,1,2,0:T(8,128)S(1)} fusion(f32[8,128,8,128]{1,3,2,0:T(8,128)S(1)} %bitcast.227), kind=kOutput, calls=%fused_computation.144 | convolution fusion | flops 1610842112 | bytes 8388608 | tf_op jit(solution)/shard_map/bu,...tu->...tb/dot_general | solution.py:49
  257.7 7.3 %fusion.92 = f32[8,128,8,128]{3,1,2,0:T(8,128)S(1)} fusion(f32[8,128,8,128]{1,3,2,0:T(8,128)S(1)} %bitcast.229), kind=kOutput, calls=%fused_computation.142 | convolution fusion | flops 1610842112 | bytes 8388608 | tf_op jit(solution)/shard_map/bu,...tu->...tb/dot_general | solution.py:50
  265.0 7.1 %convolution_subtract_fusion.1 = f32[8,128,8,128]{3,1,2,0:T(8,128)S(1)} fusion(f32[8,128,8,128]{3,1,2,0:T(8,128)S(1)} %fusion.94, f32[8,128,8,128]{1,3,2,0:T(8,128)S(1)} %bitcast.230), kind=kOutput, calls=%fused_computation.82 | convolution fusion | flops 1611890688 | bytes 12582912 | tf_op jit(solution)/shard_map/bu,...tu->...tb/dot_general | solution.py:49
  272.1 7.3 %fusion.16 = (f32[8,128,128,8]{2,1,3,0:T(8,128)S(1)}, f32[8,128,128,8]{2,1,3,0:T(8,128)S(1)}) fusion(f32[8,128,8,128]{3,1,2,0:T(8,128)S(1)} %convolution_subtract_fusion.1, f32[128,8]{0,1:T(8,128)S(1)} %get-tuple-element.27, f32[128,8]{0,1:T(8,128)S(1)} %get-tuple-element.28, f32[8,128,8,128]{3,1,2,0:T(8,128)S(1)} %fusion.92, ...), kind=kOutput, calls=%fused_computation.46 | convolution fusion | flops 1618182144 | bytes 20979712 | tf_op jit(solution)/shard_map/bu,...tu->...tb/dot_general | solution.py:50
  279.4 6.6 %fusion.28 = f32[8,128,128,8]{2,3,1,0:T(8,128)S(1)} fusion(f32[8,128,128,8]{2,1,3,0:T(8,128)S(1)} %get-tuple-element.14), kind=kOutput, calls=%fused_computation.64 | convolution fusion | flops 100664192 | bytes 8388608 | tf_op jit(solution)/shard_map/kn,...n->...k/dot_general | solution.py:49
  286.0 6.9 %subtract_bitcast_fusion = f32[8,128,8,128]{3,2,1,0:T(8,128)} fusion(f32[8,128,128,8]{2,3,1,0:T(8,128)S(1)} %fusion.28, f32[8,128,128,8]{2,1,3,0:T(8,128)S(1)} %get-tuple-element.13), kind=kOutput, calls=%fused_computation.68 | convolution fusion | flops 101712768 | bytes 12582912 | tf_op jit(solution)/shard_map/kn,...n->...k/dot_general | solution.py:49
  292.9 5.4 %copy.65 = f32[8,128,8,128]{1,3,2,0:T(8,128)} copy(f32[8,128,8,128]{3,2,1,0:T(8,128)} %subtract_bitcast_fusion) | data formatting | bytes 8388608 | tf_op jit(solution)/shard_map/reshape | solution.py:106
  298.3 4.6 copy.91
  303.1 70.2 %all_to_all.13 = f32[8,8,8192]{2,0,1:T(8,128)S(1)} all-to-all(f32[8,8,8192]{2,0,1:T(8,128)S(1)} %bitcast.240), channel_id=1, replica_groups=mesh['seq'=8,'chan'=4] {'seq'}, dimensions={1} | all-to-all | bytes 4194304 | tf_op jit(solution)/shard_map/all_to_all | solution.py:121
  373.3 9.1 %convolution_bitcast_fusion = f32[256,8192]{0,1:T(8,128)} fusion(f32[256,64]{0,1:T(8,128)S(1)} %copy-done, f32[64,8192]{1,0:T(8,128)S(1)} %copy-done.8, f32[64,8192]{1,0:T(8,128)S(1)} %copy-done.4, f32[8,8,8192]{2,0,1:T(8,128)S(1)} %all_to_all.13, f32[64]{0:T(128)S(1)} %copy-done.12), kind=kOutput, calls=%fused_computation | convolution fusion | flops 1612709888 | bytes 14745856 | tf_op jit(solution)/shard_map/dot_general | solution.py:133
  382.4 9.0 %copy.66 = f32[256,8192]{1,0:T(8,128)} copy(f32[256,8192]{0,1:T(8,128)} %convolution_bitcast_fusion) | data formatting | bytes 16777216
  391.4 70.6 %reduce-scatter.4.cloned.1.call-done = f32[64,8192]{1,0:T(8,128)} async-done(((f32[256,8192]{1,0:T(8,128)}), f32[64,8192]{1,0:T(8,128)}) %reduce-scatter.4.cloned.1.call-update) | async-done | bytes 2097168 | tf_op jit(solution)/shard_map/reduce_scatter | solution.py:132
  (64 shorter events, 43.8 us)
Async XLA Ops:
  6.5 366.8 %copy-start = (f32[256,64]{0,1:T(8,128)S(1)}, f32[256,64]{0,1:T(8,128)}, u32[]{:S(2)}) copy-start(f32[256,64]{0,1:T(8,128)} %param.13) | copy-start | bytes 196612
  6.5 12.7 %copy-start.3 = (f32[64,8192]{1,0:T(8,128)S(1)}, f32[64,8192]{1,0:T(8,128)}, u32[]{:S(2)}) copy-start(f32[64,8192]{1,0:T(8,128)} %param.9) | copy-start | bytes 6291460
  6.5 455.5 %reduce-scatter.4.cloned.1.call-start = ((), (), s32[]{:S(2)}) async-start(), calls=%async_computation.2 | async-start | bytes 10485760 | tf_op jit(solution)/shard_map/reduce_scatter | solution.py:132
  10.3 10.7 %copy-start.11 = (s32[1024]{0:T(1024)S(1)}, s32[1024]{0:T(1024)}, u32[]{:S(2)}) copy-start(s32[1024]{0:T(1024)} %constant.133.clone) | copy-start | bytes 12292
  10.3 26.9 %collective-permute-start = (f32[2,1,8,8192]{3,2,0,1:T(8,128)}, f32[2,1,8,8192]{3,2,0,1:T(8,128)}, u32[]{:S(2)}, u32[]{:S(2)}) collective-permute-start(f32[2,1,8,8192]{3,2,0,1:T(8,128)} %get-tuple-element.16), channel_id=1, source_target_pairs={{0,4},{4,0},{8,12},{12,8},{16,20},{20,16},{24,28},{28,24},{1,5},{5... | collective-permute-start | bytes 1572872 | tf_op jit(solution)/shard_map/ppermute | solution.py:23
  13.2 36.7 %collective-permute-start.1 = (f32[2,1,8,8192]{3,2,0,1:T(8,128)}, f32[2,1,8,8192]{3,2,0,1:T(8,128)}, u32[]{:S(2)}, u32[]{:S(2)}) collective-permute-start(f32[2,1,8,8192]{3,2,0,1:T(8,128)} %get-tuple-element.17), channel_id=1, source_target_pairs={{0,8},{4,12},{8,0},{12,4},{16,24},{20,28},{24,16},{28,20},{1,9},{5... | collective-permute-start | bytes 1572872 | tf_op jit(solution)/shard_map/ppermute | solution.py:23
  14.8 44.1 %collective-permute-start.2 = (f32[2,1,8,8192]{3,2,0,1:T(8,128)}, f32[2,1,8,8192]{3,2,0,1:T(8,128)}, u32[]{:S(2)}, u32[]{:S(2)}) collective-permute-start(f32[2,1,8,8192]{3,2,0,1:T(8,128)} %get-tuple-element.18), channel_id=1, source_target_pairs={{0,12},{4,8},{8,4},{12,0},{16,28},{20,24},{24,20},{28,16},{1,13},{... | collective-permute-start | bytes 1572872 | tf_op jit(solution)/shard_map/ppermute | solution.py:23
  14.8 45.1 %collective-permute-start.3 = (f32[2,1,8,8192]{3,2,0,1:T(8,128)}, f32[2,1,8,8192]{3,2,0,1:T(8,128)}, u32[]{:S(2)}, u32[]{:S(2)}) collective-permute-start(f32[2,1,8,8192]{3,2,0,1:T(8,128)} %get-tuple-element.19), channel_id=1, source_target_pairs={{0,16},{4,20},{8,24},{12,28},{16,0},{20,4},{24,8},{28,12},{1,17},{... | collective-permute-start | bytes 1572872 | tf_op jit(solution)/shard_map/ppermute | solution.py:23
  17.8 70.5 %collective-permute-start.4 = (f32[2,1,8,8192]{3,2,0,1:T(8,128)}, f32[2,1,8,8192]{3,2,0,1:T(8,128)}, u32[]{:S(2)}, u32[]{:S(2)}) collective-permute-start(f32[2,1,8,8192]{3,2,0,1:T(8,128)} %get-tuple-element.20), channel_id=1, source_target_pairs={{0,20},{4,16},{8,28},{12,24},{16,4},{20,0},{24,12},{28,8},{1,21},{... | collective-permute-start | bytes 1572872 | tf_op jit(solution)/shard_map/ppermute | solution.py:23
  23.1 1.6 copy-start.5
  28.2 8.9 %copy-start.10 = (f32[2,1,8,8192]{3,2,0,1:T(8,128)S(1)}, f32[2,1,8,8192]{3,2,0,1:T(8,128)}, u32[]{:S(2)}) copy-start(f32[2,1,8,8192]{3,2,0,1:T(8,128)} %fusion.71) | copy-start | bytes 1572868
  28.2 21.8 %copy-start.9 = (f32[2,1,8,8192]{3,2,0,1:T(8,128)S(1)}, f32[2,1,8,8192]{3,2,0,1:T(8,128)}, u32[]{:S(2)}) copy-start(f32[2,1,8,8192]{3,2,0,1:T(8,128)} %get-tuple-element.15) | copy-start | bytes 1572868
  37.1 52.3 %collective-permute-start.5 = (f32[2,1,8,8192]{3,2,0,1:T(8,128)S(1)}, f32[2,1,8,8192]{3,2,0,1:T(8,128)S(1)}, u32[]{:S(2)}, u32[]{:S(2)}) collective-permute-start(f32[2,1,8,8192]{3,2,0,1:T(8,128)S(1)} %copy-done.10), channel_id=1, source_target_pairs={{0,24},{4,28},{8,16},{12,20},{16,8},{20,12},{24,0},{28,4},{1,25},{... | collective-permute-start | bytes 1572872 | tf_op jit(solution)/shard_map/ppermute | solution.py:23
  50.0 39.5 %collective-permute-start.6 = (f32[2,1,8,8192]{3,2,0,1:T(8,128)S(1)}, f32[2,1,8,8192]{3,2,0,1:T(8,128)S(1)}, u32[]{:S(2)}, u32[]{:S(2)}) collective-permute-start(f32[2,1,8,8192]{3,2,0,1:T(8,128)S(1)} %copy-done.9), channel_id=1, source_target_pairs={{0,28},{4,24},{8,20},{12,16},{16,12},{20,8},{24,4},{28,0},{1,29},{... | collective-permute-start | bytes 1572872 | tf_op jit(solution)/shard_map/ppermute | solution.py:23
  103.7 12.3 %copy-start.1 = (f32[2,8,128,8,128]{4,3,2,1,0:T(8,128)S(1)}, f32[2,8,128,8,128]{4,3,2,1,0:T(8,128)}, u32[]{:S(2)}) copy-start(f32[2,8,128,8,128]{4,3,2,1,0:T(8,128)} %copy.64) | copy-start | bytes 25165828
  140.5 19.9 %slice-start = ((s8[8388608]{0:T(1024)(128)(4,1)}), s8[4194304]{0:T(1024)(128)(4,1)S(1)}, s32[]{:S(2)}) async-start(s8[8388608]{0:T(1024)(128)(4,1)} %bitcast.225), calls=%async_computation.3 | async-start | bytes 8388608
  151.6 8.9 %slice-start.1 = ((s8[8388608]{0:T(1024)(128)(4,1)}), s8[4194304]{0:T(1024)(128)(4,1)S(1)}, s32[]{:S(2)}) async-start(s8[8388608]{0:T(1024)(128)(4,1)} %bitcast.225), calls=%async_computation.4 | async-start | bytes 8388608
  220.2 9.6 %copy-start.2 = (f32[2,8,1024,128]{3,2,1,0:T(8,128)S(1)}, f32[2,8,1024,128]{3,2,1,0:T(8,128)}, u32[]{:S(2)}) copy-start(f32[2,8,1024,128]{3,2,1,0:T(8,128)} %convolution_subtract_fusion) | copy-start | bytes 25165828
  241.6 3.9 copy-start.6
  241.6 3.9 copy-start.7
  303.0 70.3 %copy-start.4 = (f32[64,8192]{1,0:T(8,128)S(1)}, f32[64,8192]{1,0:T(8,128)}, u32[]{:S(2)}) copy-start(f32[64,8192]{1,0:T(8,128)} %param.9) | copy-start | bytes 6291460
  303.0 70.3 %copy-start.8 = (f32[64,8192]{1,0:T(8,128)S(1)}, f32[64,8192]{1,0:T(8,128)}, u32[]{:S(2)}) copy-start(f32[64,8192]{1,0:T(8,128)} %param.10) | copy-start | bytes 6291460
  303.0 70.3 %copy-start.12 = (f32[64]{0:T(128)S(1)}, f32[64]{0:T(128)}, u32[]{:S(2)}) copy-start(f32[64]{0:T(128)} %param.12) | copy-start | bytes 772
Sparse Core Ops, SparseCore 0:
  391.5 70.4 reduce-scatter.3
